TPU v7x, 512 devices: a whole 4x4x16 slice. The times are simulated.
512 devices in a mesh: pw: 8 (over x, y_hi), band: 64 (over y_lo, z, core).
Axes of the slice: x: 4, y: 4 (y_hi: 2, y_lo: 2; y = y_hi * 2 + y_lo), z: 16, core: 2. Of those that a mesh axis runs over, the one named last changes fastest.
Arguments:
- stick_coefs: float32 [64, 8, 48, 1024], P('band', None, None, 'pw'), may hold values from -6 to 6
- miller: int32 [2, 1024], P(None, 'pw'), may hold values from 0 to 47, as said below
- stick_count: int32 [8], P('pw'), may hold values from 1 to 128, as said below
Outputs:
- exchange_coefs: float32 [64, 8, 48, 1024], P('band', None, None, 'pw')
Inputs may be any that keep to these rules, and one draw needn't show every extreme that they name: `stick_count`: some pw index has exactly 128 live sticks. Over the live slots the columns (miller[0, s], miller[1, s]) are distinct and are the columns of smallest sigma(miller[0])**2 + sigma(miller[1])**2, as many as there are live slots (ties at the edge broken arbitrarily); the other slots hold arbitrary columns.
All inputs are finite; a program needn't handle non-finite values.
Results may differ from a plain program's by a relative error of at most 0.0003.
Values sent between devices are 32-bit elements; how exact they have to be, the bound alone decides.
A program may use at most 64 MiB of HBM per device.

v0:
```python
import math

import jax
import jax.numpy as jnp
import numpy as np
from jax import lax
from jax.experimental import pallas as pl
from jax.experimental.pallas import tpu as pltpu
from jax.sharding import PartitionSpec as P

N = 48
HALF = 2
PAIRS = 2 * HALF + 1
COLS = N * N
WIDE = 256
OWNERS = 8
STK = 128
STICKS = OWNERS * STK
F32, BF16, I32 = jnp.float32, jnp.bfloat16, jnp.int32
MESH = pl.DeviceIdType.MESH
SHIFTS = (-2, -1, 1, 2)


def split_table(values):
    high = np.asarray(values, np.float32).astype(jnp.bfloat16)
    rest = np.asarray(values, np.float64) - high.astype(np.float64)
    low = rest.astype(np.float32).astype(jnp.bfloat16)
    tail = (rest - low.astype(np.float64)).astype(np.float32).astype(jnp.bfloat16)
    return high, low, tail


def constant_tables():
    index = np.arange(N)
    angles = 2.0 * math.pi / N * ((index[:, None] * index[None, :]) % N)
    cas = np.cos(angles) + np.sin(angles)
    high, low, tail = split_table(cas)
    left = np.concatenate([high, high, low], axis=1)
    exact = np.concatenate([high, low, tail], axis=1)
    block = np.kron(np.eye(PAIRS), cas)
    block = np.pad(block, ((0, WIDE - PAIRS * N), (0, WIDE - PAIRS * N)))
    turn = split_table(block)[:2]
    enter = split_table(block * N**-1.5)[:2]
    leave = np.pad(np.tile(-cas * N**-1.5, (1, PAIRS)), ((0, 0), (0, WIDE - PAIRS * N)))
    leave = split_table(leave)[:2]
    repeat = np.zeros((WIDE, WIDE))
    repeat[:N, : PAIRS * N] = np.tile(np.eye(N), (1, PAIRS))
    repeat = repeat.astype(jnp.bfloat16)
    return [np.stack([left, exact]), np.stack(turn), np.stack(enter), np.stack(leave), repeat]


def split(value):
    high = value.astype(BF16)
    low = (value - high.astype(F32)).astype(BF16)
    return high, low


def dot(a, b):
    return lax.dot_general(a, b, (((1,), (0,)), ((), ())), preferred_element_type=F32)


def dot_nt(a, b):
    return lax.dot_general(a, b, (((1,), (1,)), ((), ())), preferred_element_type=F32)


def left3(table, value):
    high, low = split(value)
    return dot(table, jnp.concatenate([high, low, high], axis=0))


def right3(value, high_t, low_t):
    high, low = split(value)
    return dot(high, high_t) + dot(low, high_t) + dot(high, low_t)


def rows_of(y, count=1):
    return pl.ds(pl.multiple_of(y * (count * N), count * N), count * N)


def screened_kernel(kern):
    lanes = lax.broadcasted_iota(I32, (1, WIDE), 1)
    kx = lanes - N * (lanes // N)
    kx = jnp.where(kx < N // 2, kx, kx - N)
    rows = lax.broadcasted_iota(I32, (N, 1), 0)
    kz = jnp.where(rows < N // 2, rows, rows - N)
    flat_q = (kz * kz + kx * kx).astype(F32)

    def slab(y, carry):
        signed = jnp.where(y < N // 2, y, y - N)
        q = flat_q + (signed * signed).astype(F32)
        scaled = jnp.maximum(q, 1.0) * (1.0 / 16.0)
        value = (4.0 / N**3) * (1.0 - jnp.exp(-scaled)) / scaled
        kern[rows_of(y), :] = jnp.where(q > 0, value, 4.0 / N**3)
        return carry

    lax.fori_loop(0, N, slab, 0)


def stick_weights(tables, left_ref, cas_y, w_hi, w_lo):
    table = jnp.concatenate([tables[q] for q in range(OWNERS)], axis=1)
    iy, iz, live = table[0:1, :], table[1:2, :], table[2:3, :]
    grid_rows = lax.broadcasted_iota(I32, (N, STICKS), 0)
    pick_y = jnp.where(grid_rows == iy, 1.0, 0.0).astype(BF16)
    pick_z = jnp.where((grid_rows == iz) & (live > 0), 1.0, 0.0).astype(BF16)
    exact = left_ref[1]
    cas_y[...] = dot(exact, jnp.concatenate([pick_y] * 3, axis=0))
    cas_z = dot(exact, jnp.concatenate([pick_z] * 3, axis=0))

    def slab(y, carry):
        high, low = split(cas_y[pl.ds(y, 1), :] * cas_z)
        w_hi[rows_of(y), :] = high
        w_lo[rows_of(y), :] = low
        return carry

    lax.fori_loop(0, N, slab, 0)


def synthesize(slots, enter_ref, w_hi, w_lo, orb):
    enter_hi, enter_lo = enter_ref[0, :, 0 : PAIRS * N], enter_ref[1, :, 0 : PAIRS * N]
    highs, lows = [], []
    for q in range(OWNERS):
        coefs = jnp.concatenate([slots[d, q] for d in range(PAIRS)], axis=0)
        high, low = split(coefs)
        lines = dot(enter_hi, high) + dot(enter_hi, low) + dot(enter_lo, high)
        high, low = split(lines)
        highs.append(high)
        lows.append(low)
    line_hi, line_lo = jnp.concatenate(highs, axis=1), jnp.concatenate(lows, axis=1)
    step = 384
    for start in range(0, COLS, step):
        wh, wl = w_hi[start : start + step, :], w_lo[start : start + step, :]
        orb[start : start + step, :] = dot_nt(wh, line_hi) + dot_nt(wh, line_lo) + dot_nt(wl, line_hi)


def pair_fields(left_ref, turn_ref, repeat_ref, orb, work0, work1, kern):
    left = left_ref[0]
    turn_hi, turn_lo = turn_ref[0], turn_ref[1]
    repeat = repeat_ref[...]
    group = 4

    def forward(i, carry):
        value = orb[rows_of(i, group), :]
        high, low = split(value)
        density = (dot(high, repeat) + dot(low, repeat)) * value
        along_x = right3(density, turn_hi, turn_lo)
        for j in range(group):
            res = left3(left, along_x[j * N : (j + 1) * N])
            y = i * group + j
            work0[pl.ds(y, N, stride=N), :] = res[:, 0:128]
            work1[pl.ds(y, N, stride=N), :] = res[:, 128:256]
        return carry

    lax.fori_loop(0, N // group, forward, 0)

    def middle(i, carry):
        for j in range(group):
            at = rows_of(i * group + j)
            value = jnp.concatenate([work0[at, :], work1[at, :]], axis=1)
            res = left3(left, value) * kern[at, :]
            res = left3(left, res)
            work0[at, :] = res[:, 0:128]
            work1[at, :] = res[:, 128:256]
        return carry

    lax.fori_loop(0, N // group, middle, 0)

    def backward(i, carry):
        parts = []
        for j in range(group):
            at = pl.ds(i * group + j, N, stride=N)
            value = jnp.concatenate([work0[at, :], work1[at, :]], axis=1)
            parts.append(left3(left, value))
        value = jnp.concatenate(parts, axis=0)
        at = rows_of(i, group)
        orb[at, :] = right3(value, turn_hi, turn_lo) * orb[at, :]
        return carry

    lax.fori_loop(0, N // group, backward, 0)


def project(leave_ref, w_hi, w_lo, orb, result):
    leave_hi, leave_lo = leave_ref[0], leave_ref[1]
    total = jnp.zeros((N, STICKS), F32)
    step = 768
    for start in range(0, COLS, step):
        high, low = split(orb[start : start + step, :])
        field = dot_nt(leave_hi, high) + dot_nt(leave_hi, low) + dot_nt(leave_lo, high)
        high, low = split(field)
        wh, wl = w_hi[start : start + step, :], w_lo[start : start + step, :]
        pieces = dot(jnp.concatenate([high, low], axis=0), wh)
        total = total + pieces[0:N] + pieces[N : 2 * N] + dot(high, wl)
    for q in range(OWNERS):
        result[q] = total[:, q * STK : (q + 1) * STK]


def everything(
    coefs_ref, table_ref, left_ref, turn_ref, enter_ref, leave_ref, repeat_ref, out_ref,
    slots, tables, w_hi, w_lo, orb, work0, work1, kern, cas_y, result,
    table_send, table_recv, deal_send, slot_recv, pass_send, back_send, back_recv, local_sem,
):
    owner = lax.axis_index("pw")
    group = lax.axis_index("band")
    groups = lax.axis_size("band")
    barrier = pltpu.get_barrier_semaphore()
    for r in range(1, OWNERS):
        pl.semaphore_signal(barrier, inc=1, device_id={"pw": (owner + r) % OWNERS}, device_id_type=MESH)
    for shift in SHIFTS:
        pl.semaphore_signal(barrier, inc=1, device_id={"band": (group + shift + groups) % groups}, device_id_type=MESH)
    keep = pltpu.make_async_copy(coefs_ref.at[0, owner], slots.at[0, owner], local_sem.at[0])
    keep.start()
    keep_table = pltpu.make_async_copy(table_ref, tables.at[owner], local_sem.at[1])
    keep_table.start()
    pl.semaphore_wait(barrier, OWNERS - 1 + len(SHIFTS))

    started = []
    for r in range(1, OWNERS):
        target = (owner + r) % OWNERS
        send = pltpu.make_async_remote_copy(
            src_ref=table_ref, dst_ref=tables.at[owner],
            send_sem=table_send.at[r - 1], recv_sem=table_recv.at[r - 1],
            device_id={"pw": target}, device_id_type=MESH)
        send.start()
        started.append(send)
        send = pltpu.make_async_remote_copy(
            src_ref=coefs_ref.at[0, target], dst_ref=slots.at[0, owner],
            send_sem=deal_send.at[r - 1], recv_sem=slot_recv.at[0, r],
            device_id={"pw": target}, device_id_type=MESH)
        send.start()
        started.append(send)

    passed = []

    def pass_on(r):
        source = (owner + OWNERS - r) % OWNERS
        for at, shift in enumerate(SHIFTS):
            send = pltpu.make_async_remote_copy(
                src_ref=slots.at[0, source], dst_ref=slots.at[at + 1, source],
                send_sem=pass_send.at[at, r], recv_sem=slot_recv.at[at + 1, r],
                device_id={"band": (group + shift + groups) % groups}, device_id_type=MESH)
            send.start()
            passed.append(send)

    keep.wait()
    pass_on(0)
    for r in range(1, OWNERS):
        started[2 * r - 1].wait_recv()
        pass_on(r)
    keep_table.wait()
    for r in range(1, OWNERS):
        started[2 * r - 2].wait_recv()

    screened_kernel(kern)
    stick_weights(tables, left_ref, cas_y, w_hi, w_lo)
    for send in passed:
        send.wait_recv()
    synthesize(slots, enter_ref, w_hi, w_lo, orb)
    pair_fields(left_ref, turn_ref, repeat_ref, orb, work0, work1, kern)
    project(leave_ref, w_hi, w_lo, orb, result)

    keep = pltpu.make_async_copy(result.at[owner], out_ref.at[0, owner], local_sem.at[0])
    keep.start()
    back = []
    for r in range(1, OWNERS):
        target = (owner + r) % OWNERS
        send = pltpu.make_async_remote_copy(
            src_ref=result.at[target], dst_ref=out_ref.at[0, owner],
            send_sem=back_send.at[r - 1], recv_sem=back_recv.at[r - 1],
            device_id={"pw": target}, device_id_type=MESH)
        send.start()
        back.append(send)
    for send in started + passed:
        send.wait_send()
    keep.wait()
    for send in back:
        send.wait()


def shards(stick_coefs, miller, stick_count):
    position = jnp.arange(STK, dtype=I32)
    live = (position < stick_count[0]).astype(I32)
    table = jnp.concatenate([miller, live[None], jnp.zeros((5, STK), I32)], axis=0)
    vmem = pl.BlockSpec(memory_space=pltpu.VMEM)
    hbm = pl.BlockSpec(memory_space=pl.ANY)
    dma = pltpu.SemaphoreType.DMA
    return pl.pallas_call(
        everything,
        out_shape=jax.ShapeDtypeStruct((1, OWNERS, N, STK), F32),
        in_specs=[hbm] + [vmem] * 6,
        out_specs=hbm,
        scratch_shapes=[
            pltpu.VMEM((PAIRS, OWNERS, N, STK), F32),
            pltpu.VMEM((OWNERS, 8, STK), I32),
            pltpu.VMEM((COLS, STICKS), BF16),
            pltpu.VMEM((COLS, STICKS), BF16),
            pltpu.VMEM((COLS, WIDE), F32),
            pltpu.VMEM((COLS, 128), F32),
            pltpu.VMEM((COLS, 128), F32),
            pltpu.VMEM((COLS, WIDE), F32),
            pltpu.VMEM((N, STICKS), F32),
            pltpu.VMEM((OWNERS, N, STK), F32),
            dma((OWNERS - 1,)),
            dma((OWNERS - 1,)),
            dma((OWNERS - 1,)),
            dma((PAIRS, OWNERS)),
            dma((PAIRS - 1, OWNERS)),
            dma((OWNERS - 1,)),
            dma((OWNERS - 1,)),
            dma((2,)),
        ],
        compiler_params=pltpu.CompilerParams(
            vmem_limit_bytes=60 * 1024 * 1024, collective_id=0, has_side_effects=True
        ),
        name="exchange",
    )(stick_coefs, table, *[jnp.asarray(t) for t in constant_tables()])


def solution(mesh):
    return jax.shard_map(
        shards,
        mesh=mesh,
        in_specs=(P("band", None, None, "pw"), P(None, "pw"), P("pw")),
        out_specs=P("band", None, None, "pw"),
        check_vma=False,
    )
```

profile of v0, /device:TPU:16, one launch (start us, length us, event | category | flops | bytes accessed | tf_op | source)
XLA Modules:
  0.0 62.7 jit_solution(1726928438053420025)
XLA Ops:
  0.7 0.0 copy-start
  0.7 0.1 pad.2.clone
  0.8 0.6 copy-done
  1.4 0.7 %add_add_fusion.table_ref = s32[8,128]{1,0:T(8,128)} fusion(s32[1,128]{1,0:T(1,128)S(1)} %compare_convert_fusion, s32[2,128]{1,0:T(2,128)S(1)} %copy-done, s32[8]{0:T(128)S(1)} %pad.2.clone), kind=kLoop, calls=%fused_computation | loop fusion | flops 2048 | bytes 5664 | tf_op jit(solution)/shard_map/concatenate | solution.py:280
  2.0 59.0 %exchange.1 = f32[1,8,48,128]{3,2,1,0:T(8,128)} custom-call(f32[1,8,48,128]{3,2,1,0:T(8,128)} %coefs_ref.1, s32[8,128]{1,0:T(8,128)} %add_add_fusion.table_ref, bf16[2,48,144]{2,1,0:T(8,128)(2,1)} %constant.12.clone.left_ref, bf16[2,256,256]{2,1,0:T(8,128)(2,1)} %constant.13.clone.turn_ref, bf16[2,256,256]{2,1,0:T(8,128)(2,1)} %constant.14.clone.enter_ref, ...), custom_call_target="tpu_custom_call" | custom-call | tf_op jit(solution)/shard_map/exchange/pallas_call | solution.py:284
  61.1 1.6 %copy.11 = f32[1,8,48,128]{3,2,1,0:T(8,128)} copy(f32[1,8,48,128]{3,2,1,0:T(8,128)} %exchange.1) | data formatting | bytes 393216
  (2 shorter events, 0.0 us)
Async XLA Ops:
  0.7 0.7 %copy-start = (s32[2,128]{1,0:T(2,128)S(1)}, s32[2,128]{1,0:T(2,128)}, u32[]{:S(2)}) copy-start(s32[2,128]{1,0:T(2,128)} %param.9) | copy-start | bytes 3076
where the time goes:
time: 62.9 us; the launch traced here: 62.7 us
  Pallas kernels  59 us (94%)
  local copies, waits for them, and re-layouts  2.29 us (4%)
  between operations  0.68 us (1%)
  other arithmetic  0.67 us (1%)
    pallas_call x1, Pallas kernels, shards(): pl.pallas_call(everything, out_shape=jax.ShapeDtypeStruct((1, OWNERS, N,...  59 us
    unnamed x3, local copies, waits for them, and re-layouts  2.22 us

commit v1 on v0

v1 whole, which is shorter than its diff:
```python
import math

import jax
import jax.numpy as jnp
import numpy as np
from jax import lax
from jax.experimental import pallas as pl
from jax.experimental.pallas import tpu as pltpu
from jax.sharding import PartitionSpec as P

N = 48
HALF = 2
PAIRS = 2 * HALF + 1
COLS = N * N
WIDE = 256
OWNERS = 8
STK = 128
STICKS = OWNERS * STK
F32, BF16, I32 = jnp.float32, jnp.bfloat16, jnp.int32
MESH = pl.DeviceIdType.MESH
SHIFTS = (-2, -1, 1, 2)


def split_table(values):
    high = np.asarray(values, np.float32).astype(jnp.bfloat16)
    rest = np.asarray(values, np.float64) - high.astype(np.float64)
    low = rest.astype(np.float32).astype(jnp.bfloat16)
    tail = (rest - low.astype(np.float64)).astype(np.float32).astype(jnp.bfloat16)
    return high, low, tail


def constant_tables():
    index = np.arange(N)
    angles = 2.0 * math.pi / N * ((index[:, None] * index[None, :]) % N)
    cas = np.cos(angles) + np.sin(angles)
    high, low, tail = split_table(cas)
    left = np.concatenate([high, high, low], axis=1)
    exact = np.concatenate([high, low, tail], axis=1)
    block = np.kron(np.eye(PAIRS), cas)
    block = np.pad(block, ((0, WIDE - PAIRS * N), (0, WIDE - PAIRS * N)))
    turn = split_table(block)[:2]
    enter = split_table(block * N**-1.5)[:2]
    leave = np.pad(np.tile(-cas * N**-1.5, (1, PAIRS)), ((0, 0), (0, WIDE - PAIRS * N)))
    leave = split_table(leave)[:2]
    return [np.stack([left, exact]), np.stack(turn), np.stack(enter), np.stack(leave)]


def split(value):
    high = value.astype(BF16)
    low = (value - high.astype(F32)).astype(BF16)
    return high, low


def dot(a, b):
    return lax.dot_general(a, b, (((1,), (0,)), ((), ())), preferred_element_type=F32)


def dot_nt(a, b):
    return lax.dot_general(a, b, (((1,), (1,)), ((), ())), preferred_element_type=F32)


def left3(table, value):
    high, low = split(value)
    return dot(table, jnp.concatenate([high, low, high], axis=0))


def right3(value, high_t, low_t):
    high, low = split(value)
    return dot(high, high_t) + dot(low, high_t) + dot(high, low_t)


def rows_of(y, count=1):
    return pl.ds(pl.multiple_of(y * (count * N), count * N), count * N)


def screened_kernel(kern):
    lanes = lax.broadcasted_iota(I32, (1, WIDE), 1)
    kx = lanes - N * (lanes // N)
    kx = jnp.where(kx < N // 2, kx, kx - N)
    rows = lax.broadcasted_iota(I32, (N, 1), 0)
    kz = jnp.where(rows < N // 2, rows, rows - N)
    flat_q = (kz * kz + kx * kx).astype(F32)

    def slab(y, carry):
        signed = jnp.where(y < N // 2, y, y - N)
        q = flat_q + (signed * signed).astype(F32)
        scaled = jnp.maximum(q, 1.0) * (1.0 / 16.0)
        value = (4.0 / N**3) * (1.0 - jnp.exp(-scaled)) / scaled
        kern[rows_of(y), :] = jnp.where(q > 0, value, 4.0 / N**3)
        return carry

    lax.fori_loop(0, N, slab, 0)


def stick_weights(tables, left_ref, cas_y, w_hi, w_lo):
    table = jnp.concatenate([tables[q] for q in range(OWNERS)], axis=1)
    iy, iz, live = table[0:1, :], table[1:2, :], table[2:3, :]
    grid_rows = lax.broadcasted_iota(I32, (N, STICKS), 0)
    pick_y = jnp.where(grid_rows == iy, 1.0, 0.0).astype(BF16)
    pick_z = jnp.where((grid_rows == iz) & (live > 0), 1.0, 0.0).astype(BF16)
    exact = left_ref[1]
    cas_y[...] = dot(exact, jnp.concatenate([pick_y] * 3, axis=0))
    cas_z = dot(exact, jnp.concatenate([pick_z] * 3, axis=0))

    def slab(y, carry):
        high, low = split(cas_y[pl.ds(y, 1), :] * cas_z)
        w_hi[rows_of(y), :] = high
        w_lo[rows_of(y), :] = low
        return carry

    lax.fori_loop(0, N, slab, 0)


def synthesize(t, slots, enter_ref, w_hi, w_lo, orb):
    enter_hi, enter_lo = enter_ref[0, :, 0 : PAIRS * N], enter_ref[1, :, 0 : PAIRS * N]
    coefs = [jnp.concatenate([slots[d, r] for d in range(PAIRS)], axis=0) for r in (2 * t, 2 * t + 1)]
    high, low = split(jnp.concatenate(coefs, axis=1))
    lines = dot(enter_hi, high) + dot(enter_hi, low) + dot(enter_lo, high)
    line_hi, line_lo = split(lines)
    cols = slice(2 * t * STK, 2 * (t + 1) * STK)
    step = 384
    for start in range(0, COLS, step):
        at = slice(start, start + step)
        wh, wl = w_hi[at, cols], w_lo[at, cols]
        part = dot_nt(wh, line_hi) + dot_nt(wh, line_lo) + dot_nt(wl, line_hi)
        orb[at, :] = part if t == 0 else orb[at, :] + part


def spread_own(value):
    own = value[:, 0:128]
    lane = lax.broadcasted_iota(I32, own.shape, 1)
    by96 = pltpu.roll(own, 96, 1)
    first = jnp.where(lane < 48, own, jnp.where(lane < 96, pltpu.roll(own, 48, 1), by96))
    second = jnp.where(lane < 16, by96, jnp.where(lane < 64, pltpu.roll(own, 16, 1), pltpu.roll(own, 64, 1)))
    return jnp.concatenate([first, second], axis=1)


GROUPS = (24, 48, 24)


def pair_fields(left_ref, turn_ref, orb, work0, work1, kern):
    left = left_ref[0]
    turn_hi, turn_lo = turn_ref[0], turn_ref[1]
    group = GROUPS[0]

    def forward(i, carry):
        value = orb[rows_of(i, group), :]
        density = spread_own(value) * value
        along_x = right3(density, turn_hi, turn_lo)
        for j in range(group):
            res = left3(left, along_x[j * N : (j + 1) * N])
            y = i * group + j
            work0[pl.ds(y, N, stride=N), :] = res[:, 0:128]
            work1[pl.ds(y, N, stride=N), :] = res[:, 128:256]
        return carry

    lax.fori_loop(0, N // group, forward, 0)
    group_m = GROUPS[1]

    def middle(i, carry):
        for j in range(group_m):
            at = rows_of(i * group_m + j)
            value = jnp.concatenate([work0[at, :], work1[at, :]], axis=1)
            res = left3(left, value) * kern[at, :]
            res = left3(left, res)
            work0[at, :] = res[:, 0:128]
            work1[at, :] = res[:, 128:256]
        return carry

    lax.fori_loop(0, N // group_m, middle, 0)
    group_b = GROUPS[2]

    def backward(i, carry):
        parts = []
        for j in range(group_b):
            at = pl.ds(i * group_b + j, N, stride=N)
            value = jnp.concatenate([work0[at, :], work1[at, :]], axis=1)
            parts.append(left3(left, value))
        value = jnp.concatenate(parts, axis=0)
        at = rows_of(i, group_b)
        orb[at, :] = right3(value, turn_hi, turn_lo) * orb[at, :]
        return carry

    lax.fori_loop(0, N // group_b, backward, 0)


def leave_grid(leave_ref, orb, field_hi, field_lo):
    leave_hi = leave_ref[0]
    both = jnp.concatenate([leave_hi, leave_ref[1]], axis=0)
    step = 768
    for start in range(0, COLS, step):
        at = slice(start, start + step)
        high, low = split(orb[at, :])
        pieces = dot_nt(both, high)
        field = pieces[0:N] + pieces[N : 2 * N] + dot_nt(leave_hi, low)
        field_hi[:, at], field_lo[:, at] = split(field)


def project(t, w_hi, w_lo, field_hi, field_lo, result):
    cols = slice(2 * t * STK, 2 * (t + 1) * STK)
    high, low = field_hi[...], field_lo[...]
    pieces = dot(jnp.concatenate([high, low], axis=0), w_hi[:, cols])
    total = pieces[0:N] + pieces[N : 2 * N] + dot(high, w_lo[:, cols])
    result[2 * t] = total[:, 0:STK]
    result[2 * t + 1] = total[:, STK : 2 * STK]


def everything(
    coefs_ref, miller_ref, count_ref, left_src, turn_src, enter_src, leave_src, out_ref,
    slots, tables, w_hi, w_lo, orb, work0, work1, kern, cas_y, field_hi, field_lo, result, mine,
    left_ref, turn_ref, enter_ref, leave_ref,
    table_send, table_recv, deal_send, slot_recv, pass_send, back_send, back_recv, local_sem,
):
    owner = lax.axis_index("pw")
    group = lax.axis_index("band")
    groups = lax.axis_size("band")
    side = 1 - 2 * (group % 2)
    partner = (group + side + groups) % groups
    near = (group - side + groups) % groups
    far = (group + 2 * side + groups) % groups
    barrier = pltpu.get_barrier_semaphore()
    for r in range(1, OWNERS):
        pl.semaphore_signal(barrier, inc=1, device_id={"pw": (owner + r) % OWNERS}, device_id_type=MESH)
    for shift in SHIFTS:
        pl.semaphore_signal(barrier, inc=1, device_id={"band": (group + shift + groups) % groups}, device_id_type=MESH)
    keep = pltpu.make_async_copy(coefs_ref.at[0, owner], slots.at[0, 0], local_sem.at[0])
    keep.start()
    loads = []
    for at, (src, dst) in enumerate(
        ((left_src, left_ref), (enter_src, enter_ref), (turn_src, turn_ref), (leave_src, leave_ref))
    ):
        load = pltpu.make_async_copy(src, dst, local_sem.at[at + 1])
        load.start()
        loads.append(load)
    live = jnp.where(lax.broadcasted_iota(I32, (1, STK), 1) < count_ref[0], 1, 0)
    my_table = jnp.concatenate([miller_ref[...], live, jnp.zeros((5, STK), I32)], axis=0)
    mine[...] = my_table
    tables[0] = my_table
    pl.semaphore_wait(barrier, OWNERS - 1 + len(SHIFTS))

    table_sends, deals = [], []
    for r in range(1, OWNERS):
        send = pltpu.make_async_remote_copy(
            src_ref=mine, dst_ref=tables.at[r],
            send_sem=table_send.at[r - 1], recv_sem=table_recv.at[r - 1],
            device_id={"pw": (owner + r) % OWNERS}, device_id_type=MESH)
        send.start()
        table_sends.append(send)
    for r in range(1, OWNERS):
        target = (owner + r) % OWNERS
        send = pltpu.make_async_remote_copy(
            src_ref=coefs_ref.at[0, target], dst_ref=slots.at[0, r],
            send_sem=deal_send.at[r - 1], recv_sem=slot_recv.at[0, r],
            device_id={"pw": target}, device_id_type=MESH)
        send.start()
        deals.append(send)

    passed = {}

    def hand(slot, r, source, target):
        send = pltpu.make_async_remote_copy(
            src_ref=slots.at[source, r], dst_ref=slots.at[slot, r],
            send_sem=pass_send.at[slot - 1, r], recv_sem=slot_recv.at[slot, r],
            device_id={"band": target}, device_id_type=MESH)
        send.start()
        passed[slot, r] = send

    def pass_on(r):
        hand(2, r, 0, near)
        hand(3, r, 0, far)
        hand(1, r, 0, partner)

    keep.wait()
    pass_on(0)
    screened_kernel(kern)
    for r in range(1, OWNERS):
        deals[r - 1].wait_recv()
        pass_on(r)
    for send in table_sends:
        send.wait_recv()
    for load in loads:
        load.wait()
    stick_weights(tables, left_ref, cas_y, w_hi, w_lo)
    for t in range(OWNERS // 2 + 1):
        if t < OWNERS // 2:
            for r in (2 * t, 2 * t + 1):
                passed[2, r].wait_recv()
                hand(4, r, 2, partner)
        if t > 0:
            for slot in (1, 3, 4):
                for r in (2 * t - 2, 2 * t - 1):
                    passed[slot, r].wait_recv()
            synthesize(t - 1, slots, enter_ref, w_hi, w_lo, orb)
    pair_fields(left_ref, turn_ref, orb, work0, work1, kern)
    leave_grid(leave_ref, orb, field_hi, field_lo)

    back = []
    for t in (1, 2, 3, 0):
        project(t, w_hi, w_lo, field_hi, field_lo, result)
        for r in (2 * t, 2 * t + 1):
            if r == 0:
                keep = pltpu.make_async_copy(result.at[0], out_ref.at[0, owner], local_sem.at[0])
                keep.start()
                continue
            source = (owner + OWNERS - r) % OWNERS
            send = pltpu.make_async_remote_copy(
                src_ref=result.at[r], dst_ref=out_ref.at[0, owner],
                send_sem=back_send.at[r - 1], recv_sem=back_recv.at[r - 1],
                device_id={"pw": source}, device_id_type=MESH)
            send.start()
            back.append(send)
    for send in table_sends + deals + list(passed.values()):
        send.wait_send()
    keep.wait()
    for send in back:
        send.wait()


def shards(stick_coefs, miller, stick_count):
    vmem = pl.BlockSpec(memory_space=pltpu.VMEM)
    smem = pl.BlockSpec(memory_space=pltpu.SMEM)
    hbm = pl.BlockSpec(memory_space=pl.ANY)
    dma = pltpu.SemaphoreType.DMA
    consts = [jnp.asarray(t) for t in constant_tables()]
    return pl.pallas_call(
        everything,
        out_shape=jax.ShapeDtypeStruct((1, OWNERS, N, STK), F32),
        in_specs=[hbm, vmem, smem] + [hbm] * 4,
        out_specs=hbm,
        scratch_shapes=[
            pltpu.VMEM((PAIRS, OWNERS, N, STK), F32),
            pltpu.VMEM((OWNERS, 8, STK), I32),
            pltpu.VMEM((COLS, STICKS), BF16),
            pltpu.VMEM((COLS, STICKS), BF16),
            pltpu.VMEM((COLS, WIDE), F32),
            pltpu.VMEM((COLS, 128), F32),
            pltpu.VMEM((COLS, 128), F32),
            pltpu.VMEM((COLS, WIDE), F32),
            pltpu.VMEM((N, STICKS), F32),
            pltpu.VMEM((N, COLS), BF16),
            pltpu.VMEM((N, COLS), BF16),
            pltpu.VMEM((OWNERS, N, STK), F32),
            pltpu.VMEM((8, STK), I32),
        ]
        + [pltpu.VMEM(t.shape, t.dtype) for t in consts]
        + [
            dma((OWNERS - 1,)),
            dma((OWNERS - 1,)),
            dma((OWNERS - 1,)),
            dma((PAIRS, OWNERS)),
            dma((PAIRS - 1, OWNERS)),
            dma((OWNERS - 1,)),
            dma((OWNERS - 1,)),
            dma((5,)),
        ],
        compiler_params=pltpu.CompilerParams(
            vmem_limit_bytes=60 * 1024 * 1024, collective_id=0, has_side_effects=True
        ),
        name="exchange",
    )(stick_coefs, miller, stick_count, *consts)


def solution(mesh):
    return jax.shard_map(
        shards,
        mesh=mesh,
        in_specs=(P("band", None, None, "pw"), P(None, "pw"), P("pw")),
        out_specs=P("band", None, None, "pw"),
        check_vma=False,
    )
```

time: 62.9 us -> 47.1 us (0.75)
  the two profiles are of different devices: /device:TPU:16 before, /device:TPU:1 now
where the time goes in v1:
time: 47.1 us; the launch traced here: 46.9 us
  Pallas kernels  44.7 us (95%)
  local copies, waits for them, and re-layouts  1.62 us (3%)
  between operations  0.66 us (1%)
    pallas_call x1, Pallas kernels, shards(): pl.pallas_call(everything, out_shape=jax.ShapeDtypeStruct((1, OWNERS, N,...  44.7 us
    unnamed x1, local copies, waits for them, and re-layouts  1.62 us

profile of v1, /device:TPU:1, one launch (start us, length us, event | category | flops | bytes accessed | tf_op | source)
XLA Modules:
  0.0 46.9 jit_solution(17218992835928794199)
XLA Ops:
  0.7 44.7 %exchange.1 = f32[1,8,48,128]{3,2,1,0:T(8,128)} custom-call(f32[1,8,48,128]{3,2,1,0:T(8,128)} %coefs_ref.1, s32[2,128]{1,0:T(2,128)} %miller_ref.1, s32[1]{0:T(128)S(6)} %copy.9.count_ref, bf16[2,48,144]{2,1,0:T(8,128)(2,1)} %constant.8.clone.left_src, bf16[2,256,256]{2,1,0:T(8,128)(2,1)} %constant.9.clone.turn_src, ...), custom_call_target="tpu_custom_call" | custom-call | tf_op jit(solution)/shard_map/exchange/pallas_call | solution.py:325
  45.3 1.6 %copy.10 = f32[1,8,48,128]{3,2,1,0:T(8,128)} copy(f32[1,8,48,128]{3,2,1,0:T(8,128)} %exchange.1) | data formatting | bytes 393216

commit v2 on v1

--- a/solution.py
+++ b/solution.py
@@ -281,16 +281,14 @@
     for load in loads:
         load.wait()
     stick_weights(tables, left_ref, cas_y, w_hi, w_lo)
-    for t in range(OWNERS // 2 + 1):
-        if t < OWNERS // 2:
+    for r in range(OWNERS):
+        passed[2, r].wait_recv()
+        hand(4, r, 2, partner)
+    for t in range(OWNERS // 2):
+        for slot in (1, 3, 4):
             for r in (2 * t, 2 * t + 1):
-                passed[2, r].wait_recv()
-                hand(4, r, 2, partner)
-        if t > 0:
-            for slot in (1, 3, 4):
-                for r in (2 * t - 2, 2 * t - 1):
-                    passed[slot, r].wait_recv()
-            synthesize(t - 1, slots, enter_ref, w_hi, w_lo, orb)
+                passed[slot, r].wait_recv()
+        synthesize(t, slots, enter_ref, w_hi, w_lo, orb)
     pair_fields(left_ref, turn_ref, orb, work0, work1, kern)
     leave_grid(leave_ref, orb, field_hi, field_lo)
 

time: 47.1 us -> 47 us (level)
  the two profiles are of different devices: /device:TPU:1 before, /device:TPU:2 now
where the time goes in v2:
time: 47 us; the launch traced here: 46.9 us
  Pallas kernels  44.6 us (95%)
  local copies, waits for them, and re-layouts  1.62 us (3%)
  between operations  0.66 us (1%)
    pallas_call x1, Pallas kernels, shards(): pl.pallas_call(everything, out_shape=jax.ShapeDtypeStruct((1, OWNERS, N,...  44.6 us
    unnamed x1, local copies, waits for them, and re-layouts  1.62 us

profile of v2, /device:TPU:2, one launch (start us, length us, event | category | flops | bytes accessed | tf_op | source)
XLA Modules:
  0.0 46.9 jit_solution(18401887808284480268)
XLA Ops:
  0.7 44.6 %exchange.1 = f32[1,8,48,128]{3,2,1,0:T(8,128)} custom-call(f32[1,8,48,128]{3,2,1,0:T(8,128)} %coefs_ref.1, s32[2,128]{1,0:T(2,128)} %miller_ref.1, s32[1]{0:T(128)S(6)} %copy.9.count_ref, bf16[2,48,144]{2,1,0:T(8,128)(2,1)} %constant.8.clone.left_src, bf16[2,256,256]{2,1,0:T(8,128)(2,1)} %constant.9.clone.turn_src, ...), custom_call_target="tpu_custom_call" | custom-call | tf_op jit(solution)/shard_map/exchange/pallas_call | solution.py:323
  45.3 1.6 %copy.10 = f32[1,8,48,128]{3,2,1,0:T(8,128)} copy(f32[1,8,48,128]{3,2,1,0:T(8,128)} %exchange.1) | data formatting | bytes 393216
